TPU v7x, 32 devices: a whole 2x2x4 slice. The times are simulated.
32 devices in a mesh: section: 1, dp: 32 (over z, y, x, core).
Axes of the slice: x: 2, y: 2, z: 4, core: 2. Of those that a mesh axis runs over, the one named last changes fastest.
Arguments:
- tokens: bfloat16 [4096, 8192], P('dp'), may hold values from -6 to 6
- blocks_in: bfloat16 [1, 160, 128, 128], P('section', 'dp'), may hold values from -0.078125 to 0.078125
- blocks_out: bfloat16 [1, 160, 128, 128], P('section', 'dp'), may hold values from -0.3125 to 0.3125
- pos_in: int32 [1, 160], P('section', 'dp'), may hold values from 0 to 256, as said below
- pos_out: int32 [1, 160], P('section', 'dp'), may hold values from 0 to 256, as said below
- cotangent: bfloat16 [4096, 8192], P('dp'), may hold values from -0.08984375 to 0.08984375
Outputs:
- grad_in: bfloat16 [1, 160, 128, 128], P('section', 'dp')
- grad_out: bfloat16 [1, 160, 128, 128], P('section', 'dp')
Inputs may be any that keep to these rules, and one draw needn't show every extreme that they name: For each layer the first k slots (k from 110 to 160) hold distinct block numbers and the other slots hold 256, marking an empty slot; in each of pos_in and pos_out some layer fills all 160 slots. `pos_out`: as for pos_in, drawn independently.
All inputs are finite; a program needn't handle non-finite values.
Results may differ from a plain program's by a relative error of at most 0.023.
Values may be sent and summed in bfloat16 or wider, within the bound.
A program may use at most 128 MiB of HBM per device.

v0:
```python
import jax
import jax.numpy as jnp
from jax import lax
from jax.sharding import PartitionSpec as P

D = 8192
RANK = 512
BLOCK = 128
MICRO = 2


EPS = 1e-05


def from_behind(block, axis, distance):
    devices = range(lax.axis_size(axis))
    route = [(i - distance, i) for i in devices if i - distance in devices]
    return lax.ppermute(block, axis, route)


def expand(blocks, places, rows_b, cols_b):
    flat = jnp.zeros((rows_b * cols_b, BLOCK, BLOCK), blocks.dtype)
    flat = flat.at[places].set(blocks, mode="drop")
    return (
        flat.reshape(rows_b, cols_b, BLOCK, BLOCK)
        .transpose(0, 2, 1, 3)
        .reshape(rows_b * BLOCK, cols_b * BLOCK)
    )


def slot_grads(left, right, places, rows_b, cols_b):
    count = left.shape[0]
    valid = places < rows_b * cols_b
    row_block = jnp.where(valid, places // cols_b, 0).astype(jnp.int32)
    col_block = jnp.where(valid, places % cols_b, 0).astype(jnp.int32)
    left_blocks = jnp.take(left.reshape(count, rows_b, BLOCK), row_block, axis=1)
    right_blocks = jnp.take(right.reshape(count, cols_b, BLOCK), col_block, axis=1)
    result = jnp.einsum(
        "tjb,tjc->jbc", left_blocks, right_blocks, preferred_element_type=jnp.float32
    )
    return jnp.where(valid[:, None, None], result, 0.0)


def norm_parts(hidden):
    wide = hidden.astype(jnp.float32)
    scale = jnp.sqrt(jnp.mean(wide * wide, axis=-1, keepdims=True) + EPS)
    return (wide, scale)


def forward_layer(hidden, mat_a, mat_b):
    wide, scale = norm_parts(hidden)
    normed = (wide / scale).astype(jnp.bfloat16)
    pre = jnp.dot(normed, mat_a, preferred_element_type=jnp.float32)
    act = (pre * jax.nn.sigmoid(pre)).astype(jnp.bfloat16)
    return (wide + jnp.dot(act, mat_b, preferred_element_type=jnp.float32)).astype(jnp.bfloat16)


def backward_layer(hidden, upstream, mat_a, mat_b):
    wide, scale = norm_parts(hidden)
    unit = wide / scale
    normed = unit.astype(jnp.bfloat16)
    pre = jnp.dot(normed, mat_a, preferred_element_type=jnp.float32)
    sig = jax.nn.sigmoid(pre)
    act = (pre * sig).astype(jnp.bfloat16)
    dact = lax.dot_general(
        upstream, mat_b, (((1,), (1,)), ((), ())), preferred_element_type=jnp.float32
    )
    dpre = (dact * sig * (1.0 + pre * (1.0 - sig))).astype(jnp.bfloat16)
    dnorm = lax.dot_general(
        dpre, mat_a, (((1,), (1,)), ((), ())), preferred_element_type=jnp.float32
    )
    inner = jnp.mean(dnorm * unit, axis=-1, keepdims=True)
    earlier = (upstream.astype(jnp.float32) + (dnorm - unit * inner) / scale).astype(jnp.bfloat16)
    return (earlier, normed, dpre, act)


def store(stack, value, picked, active):
    updated = lax.dynamic_update_slice_in_dim(stack, value[None], picked, 0)
    return jnp.where(active, updated, stack)


def per_device(tokens, blocks_in, blocks_out, pos_in, pos_out, cotangent):
    sections = lax.axis_size("section")
    here = lax.axis_index("section")
    rows_d = D // BLOCK
    rows_k = RANK // BLOCK
    full_in, full_out, all_in, all_out = (
        lax.all_gather(blocks_in, "dp", axis=1, tiled=True),
        lax.all_gather(blocks_out, "dp", axis=1, tiled=True),
        lax.all_gather(pos_in, "dp", axis=1, tiled=True),
        lax.all_gather(pos_out, "dp", axis=1, tiled=True),
    )
    mat_a = expand(full_in[0], all_in[0], rows_d, rows_k)
    mat_b = expand(full_out[0], all_out[0], rows_k, rows_d)
    micro_rows = tokens.shape[0] // MICRO
    turns = MICRO + sections - 1
    saved = jnp.zeros((MICRO, micro_rows, D), jnp.bfloat16)
    carried = jnp.zeros((micro_rows, D), jnp.bfloat16)
    for turn in range(turns):
        micro = turn - here
        active = (micro >= 0) & (micro < MICRO)
        picked = jnp.clip(micro, 0, MICRO - 1)
        first = lax.dynamic_slice_in_dim(tokens, picked * micro_rows, micro_rows, 0)
        entering = jnp.where(here == 0, first, carried)
        saved = store(saved, entering, picked, active)
        if turn < turns - 1:
            leaving = lax.cond(
                active, lambda x: forward_layer(x, mat_a, mat_b), lambda x: x, entering
            )
            carried = from_behind(leaving, "section", 1)
    kept_normed = jnp.zeros((MICRO, micro_rows, D), jnp.bfloat16)
    kept_dpre = jnp.zeros((MICRO, micro_rows, RANK), jnp.bfloat16)
    kept_act = jnp.zeros((MICRO, micro_rows, RANK), jnp.bfloat16)
    kept_upper = jnp.zeros((MICRO, micro_rows, D), jnp.bfloat16)
    carried_grad = jnp.zeros((micro_rows, D), jnp.bfloat16)
    for turn in range(turns):
        micro = turn - (sections - 1 - here)
        active = (micro >= 0) & (micro < MICRO)
        picked = jnp.clip(micro, 0, MICRO - 1)
        last = lax.dynamic_slice_in_dim(cotangent, picked * micro_rows, micro_rows, 0)
        upstream = jnp.where(here == sections - 1, last, carried_grad)
        hidden = lax.dynamic_index_in_dim(saved, picked, 0, keepdims=False)

        def run_layer():
            return backward_layer(hidden, upstream, mat_a, mat_b)

        def skip_layer():
            return (
                upstream,
                jnp.zeros((micro_rows, D), jnp.bfloat16),
                jnp.zeros((micro_rows, RANK), jnp.bfloat16),
                jnp.zeros((micro_rows, RANK), jnp.bfloat16),
            )

        earlier, normed, dpre, act = lax.cond(active, run_layer, skip_layer)
        kept_normed = store(kept_normed, normed, picked, active)
        kept_dpre = store(kept_dpre, dpre, picked, active)
        kept_act = store(kept_act, act, picked, active)
        kept_upper = store(kept_upper, upstream, picked, active)
        if turn < turns - 1:
            carried_grad = from_behind(earlier, "section", -1)
    all_rows = MICRO * micro_rows
    terms_in = slot_grads(
        kept_normed.reshape(all_rows, D),
        kept_dpre.reshape(all_rows, RANK),
        all_in[0],
        rows_d,
        rows_k,
    )[None]
    terms_out = slot_grads(
        kept_act.reshape(all_rows, RANK),
        kept_upper.reshape(all_rows, D),
        all_out[0],
        rows_k,
        rows_d,
    )[None]
    sums_in, sums_out = (
        lax.psum_scatter(
            terms_in.astype(jnp.bfloat16), "dp", scatter_dimension=1, tiled=True
        ).astype(jnp.float32),
        lax.psum_scatter(
            terms_out.astype(jnp.bfloat16), "dp", scatter_dimension=1, tiled=True
        ).astype(jnp.float32),
    )
    return (sums_in.astype(jnp.bfloat16), sums_out.astype(jnp.bfloat16))


def solution(mesh):
    in_specs = (
        P("dp", None),
        P("section", "dp", None, None),
        P("section", "dp", None, None),
        P("section", "dp"),
        P("section", "dp"),
        P("dp", None),
    )
    out_specs = (P("section", "dp", None, None), P("section", "dp", None, None))
    return jax.shard_map(
        per_device, mesh=mesh, in_specs=in_specs, out_specs=out_specs, check_vma=False
    )
```

profile of v0, /device:TPU:0, one launch (start us, length us, event | category | flops | bytes accessed | tf_op | source)
XLA Modules:
  0.0 452.2 jit_solution(7334522181519335815)
XLA Ops:
  7.2 0.0 all-gather.5.cloned.1.call-start
  7.2 0.7 all-gather.5.cloned.1.call-update
  7.9 0.0 all-gather.3.cloned.1.call-start
  7.9 0.7 all-gather.3.cloned.1.call-update
  8.6 0.0 reduce-scatter.5.cloned.1.call-start
  8.7 1.7 slice_bitcast_fusion.1
  10.4 0.2 pad_maximum_fusion.1
  10.6 0.0 copy-start.4
  10.6 0.0 copy-start.5
  10.6 0.6 copy.35
  11.2 1.4 copy.28
  12.6 0.0 copy-done.4
  12.6 0.1 bitcast_dynamic-update-slice_fusion
  12.7 0.0 copy-done.5
  12.7 0.1 bitcast_dynamic-update-slice_fusion.1
  12.8 42.2 %all-reduce.2 = (s32[160]{0:T(256)S(1)}, s32[160]{0:T(256)S(1)}) all-reduce(s32[160]{0:T(256)S(1)} %bitcast_dynamic-update-slice_fusion.1, s32[160]{0:T(256)S(1)} %bitcast_dynamic-update-slice_fusion), channel_id=1, replica_groups=mesh['section'=1,'dp'=32] {'dp'}, use_global_device_ids=true, to_apply=%add | all-reduce | flops 320 | bytes 2560 | tf_op jit(solution)/shard_map/squeeze | solution.py:146
  55.0 7.8 %gather_fusion.3 = bf16[160,128,128]{2,1,0:T(8,128)(2,1)} fusion(bf16[128,64,128]{2,0,1:T(8,128)(2,1)S(1)} %copy.28, s32[1024]{0:T(1024)S(1)} %pad_clamp_fusion), kind=kCustom, calls=%fused_computation.2.clone | custom fusion | bytes 10486400 | tf_op jit(solution)/shard_map/jit(_take)/gather | solution.py:37
  62.8 2.1 fusion.38
  64.9 14.1 %all-gather.5.cloned.1.call-done = bf16[1,160,128,128]{3,2,0,1:T(8,128)(2,1)} async-done(((bf16[1,5,128,128]{3,2,0,1:T(8,128)(2,1)}), bf16[1,160,128,128]{3,2,0,1:T(8,128)(2,1)}) %all-gather.5.cloned.1.call-update) | async-done | bytes 5242896 | tf_op jit(solution)/shard_map/all_gather | solution.py:88
  79.0 5.4 %broadcast.170.clone.1 = bf16[256,128,128]{2,1,0:T(8,128)(2,1)} broadcast(bf16[]{:T(256)} %constant.170.clone.1), dimensions={} | broadcast | bytes 8388610 | tf_op jit(solution)/shard_map/broadcast.39
  84.3 24.1 %scatter_fusion.1 = bf16[256,128,128]{2,1,0:T(8,128)(2,1)} fusion(bf16[256,128,128]{2,1,0:T(8,128)(2,1)} %broadcast.170.clone.1, s32[160]{0:T(256)S(1)} %bitcast.134, bf16[160,128,128]{2,1,0:T(8,128)(2,1)} %bitcast.131), kind=kCustom, calls=%fused_computation.5 | custom fusion | bytes 15729280 | tf_op jit(solution)/shard_map/scatter | solution.py:23
  108.4 0.0 copy-start
  108.4 12.3 %copy.24 = bf16[64,128,4,128]{1,0,3,2:T(8,128)(2,1)} copy(bf16[64,128,4,128]{3,1,2,0:T(8,128)(2,1)} %bitcast.121) | data formatting | bytes 16777216 | tf_op jit(solution)/shard_map/transpose | solution.py:26
  120.7 0.0 copy-done
  120.7 0.0 copy-start.1
  120.7 12.3 %fusion.2 = f32[64,512]{1,0:T(8,128)S(1)} fusion(bf16[64,8,64,128]{3,2,1,0:T(8,128)(2,1)} %bitcast.122, f32[64]{0:T(128)S(1)} %get-tuple-element.57, bf16[128,8192]{1,0:T(8,128)(2,1)S(1)} %copy-done), kind=kOutput, calls=%fused_computation.10 | convolution fusion | flops 538443776 | bytes 9568768 | tf_op jit(solution)/shard_map/cond/branch_1_fun/dot_general | solution.py:62
  133.1 0.0 copy-done.1
  133.1 9.0 %fusion = f32[64,512]{1,0:T(8,128)S(1)} fusion(bf16[64,8,64,128]{3,2,1,0:T(8,128)(2,1)S(1)} %bitcast.123, f32[64]{0:T(128)S(1)} %get-tuple-element.56, bf16[128,8192]{1,0:T(8,128)(2,1)S(1)} %copy-done), kind=kOutput, calls=%fused_computation.8 | convolution fusion | flops 538443776 | bytes 9568768 | tf_op jit(solution)/shard_map/cond/branch_1_fun/dot_general | solution.py:62
  142.3 7.6 %gather_fusion.2 = bf16[160,128,128]{2,1,0:T(8,128)(2,1)} fusion(bf16[128,4,128]{2,0,1:T(8,128)(2,1)S(1)} %copy.27, s32[1024]{0:T(1024)S(1)} %pad_clamp_fusion.1), kind=kCustom, calls=%fused_computation.3.clone | custom fusion | bytes 10486400 | tf_op jit(solution)/shard_map/jit(_take)/gather | solution.py:36
  149.9 9.5 %fusion.13 = bf16[1,160,128,128]{3,2,1,0:T(8,128)(2,1)} fusion(pred[160]{0:T(512)(128)(4,1)S(1)} %get-tuple-element.45, bf16[160,128,128]{2,1,0:T(8,128)(2,1)} %gather_fusion.3, pred[160]{0:T(512)(128)(4,1)S(1)} %get-tuple-element.46, bf16[160,128,128]{2,1,0:T(8,128)(2,1)} %gather_fusion.2, pred[160]{0:T(512)(128)(4,1)S(1)} %get-tuple-element.33), kind=kOutput, calls=%fused_computation.21 | convolution fusion | flops 681574400 | bytes 15729120 | tf_op jit(solution)/shard_map/tjb,tjc->jbc/dot_general | solution.py:38
  159.4 0.0 reduce-scatter.5.cloned.1.call-update
  159.4 0.0 reduce-scatter.3.cloned.1.call-start
  159.4 0.5 fusion.83
  159.9 0.2 pad_maximum_fusion
  160.1 0.6 copy.32
  160.7 1.4 copy.20
  162.1 7.8 %gather_fusion = bf16[160,128,128]{2,1,0:T(8,128)(2,1)} fusion(bf16[128,64,128]{2,0,1:T(8,128)(2,1)S(1)} %copy.20, s32[1024]{0:T(1024)S(1)} %pad_clamp_fusion.3), kind=kCustom, calls=%fused_computation.clone | custom fusion | bytes 10486400 | tf_op jit(solution)/shard_map/jit(_take)/gather | solution.py:36
  169.9 0.0 all-gather.3.cloned.1.call-done
  169.9 5.4 %broadcast.170.clone = bf16[256,128,128]{2,1,0:T(8,128)(2,1)} broadcast(bf16[]{:T(256)} %constant.170.clone.1), dimensions={} | broadcast | bytes 8388610 | tf_op jit(solution)/shard_map/broadcast.39
  175.3 24.3 %scatter_fusion = bf16[256,128,128]{2,1,0:T(8,128)(2,1)} fusion(bf16[256,128,128]{2,1,0:T(8,128)(2,1)} %broadcast.170.clone, s32[160]{0:T(256)S(1)} %bitcast.135, bf16[160,128,128]{2,1,0:T(8,128)(2,1)} %bitcast.130), kind=kCustom, calls=%fused_computation.4 | custom fusion | bytes 15729280 | tf_op jit(solution)/shard_map/scatter | solution.py:23
  199.6 0.0 copy-start.3
  199.6 12.2 %copy.22 = bf16[4,128,64,128]{3,2,1,0:T(8,128)(2,1)} copy(bf16[4,128,64,128]{3,1,2,0:T(8,128)(2,1)} %bitcast.120) | data formatting | bytes 16777216 | tf_op jit(solution)/shard_map/transpose | solution.py:26
  211.8 0.0 copy-done.3
  211.8 0.0 copy-start.2
  211.8 12.2 %fusion.69 = bf16[1,64,512]{2,1,0:T(8,128)(2,1)S(1)} fusion(bf16[64,8,64,128]{3,2,1,0:T(8,128)(2,1)} %bitcast.124, bf16[128,8192]{1,0:T(8,128)(2,1)S(1)} %copy-done.3, f32[64,512]{1,0:T(8,128)S(1)} %fusion.2), kind=kOutput, calls=%fused_computation.57 | convolution fusion | flops 537165824 | bytes 9633792 | tf_op jit(solution)/shard_map/cond/branch_1_fun/dot_general | solution.py:65
  224.0 0.0 copy-done.2
  224.0 8.4 %fusion.66 = bf16[1,64,512]{2,1,0:T(8,128)(2,1)S(1)} fusion(bf16[64,8,64,128]{3,2,1,0:T(8,128)(2,1)S(1)} %bitcast.125, bf16[128,8192]{1,0:T(8,128)(2,1)S(1)} %copy-done.3, f32[64,512]{1,0:T(8,128)S(1)} %fusion), kind=kOutput, calls=%fused_computation.56 | convolution fusion | flops 537165824 | bytes 9633792 | tf_op jit(solution)/shard_map/cond/branch_1_fun/dot_general | solution.py:65
  232.5 7.9 %gather_fusion.1 = bf16[160,128,128]{2,1,0:T(8,128)(2,1)} fusion(bf16[128,4,128]{2,0,1:T(8,128)(2,1)S(1)} %copy.25, s32[1024]{0:T(1024)S(1)} %pad_clamp_fusion.2), kind=kCustom, calls=%fused_computation.1.clone | custom fusion | bytes 10486400 | tf_op jit(solution)/shard_map/jit(_take)/gather | solution.py:37
  240.3 9.6 %fusion.12 = bf16[1,160,128,128]{3,2,1,0:T(8,128)(2,1)} fusion(pred[160]{0:T(512)(128)(4,1)S(1)} %get-tuple-element.53, bf16[160,128,128]{2,1,0:T(8,128)(2,1)} %gather_fusion.1, pred[160]{0:T(512)(128)(4,1)S(1)} %get-tuple-element.51, bf16[160,128,128]{2,1,0:T(8,128)(2,1)} %gather_fusion, pred[160]{0:T(512)(128)(4,1)S(1)} %get-tuple-element.54), kind=kOutput, calls=%fused_computation.20 | convolution fusion | flops 681574400 | bytes 15729120 | tf_op jit(solution)/shard_map/tjb,tjc->jbc/dot_general | solution.py:38
  249.9 0.0 reduce-scatter.3.cloned.1.call-update
  249.9 52.5 %reduce-scatter.5.cloned.1.call-done = bf16[1,5,128,128]{3,2,1,0:T(8,128)(2,1)} async-done(((bf16[1,160,128,128]{3,2,1,0:T(8,128)(2,1)}), bf16[1,5,128,128]{3,2,1,0:T(8,128)(2,1)}) %reduce-scatter.5.cloned.1.call-update) | async-done | bytes 163856 | tf_op jit(solution)/shard_map/reduce_scatter | solution.py:161
  302.4 142.8 %reduce-scatter.3.cloned.1.call-done = bf16[1,5,128,128]{3,2,1,0:T(8,128)(2,1)} async-done(((bf16[1,160,128,128]{3,2,1,0:T(8,128)(2,1)}), bf16[1,5,128,128]{3,2,1,0:T(8,128)(2,1)}) %reduce-scatter.3.cloned.1.call-update) | async-done | bytes 163856 | tf_op jit(solution)/shard_map/reduce_scatter | solution.py:158
  (18 shorter events, 0.3 us)
Async XLA Ops:
  7.2 71.8 %all-gather.5.cloned.1.call-start = ((), (), s32[]{:S(2)}) async-start(), calls=%async_computation.3 | async-start | bytes 5406720 | tf_op jit(solution)/shard_map/all_gather | solution.py:88
  7.9 162.0 %all-gather.3.cloned.1.call-start = ((), (), s32[]{:S(2)}) async-start(), calls=%async_computation.2 | async-start | bytes 5406720 | tf_op jit(solution)/shard_map/all_gather | solution.py:89
  8.6 293.8 %reduce-scatter.5.cloned.1.call-start = ((), (), s32[]{:S(2)}) async-start(), calls=%async_computation.5 | async-start | bytes 5406720 | tf_op jit(solution)/shard_map/reduce_scatter | solution.py:161
  10.6 2.0 copy-start.4
  10.6 2.1 copy-start.5
  108.4 12.3 %copy-start = (bf16[128,8192]{1,0:T(8,128)(2,1)S(1)}, bf16[128,8192]{1,0:T(8,128)(2,1)}, u32[]{:S(2)}) copy-start(bf16[128,8192]{1,0:T(8,128)(2,1)} %param.10) | copy-start | bytes 6291460
  120.7 12.4 %copy-start.1 = (bf16[64,128,4,128]{1,0,3,2:T(8,128)(2,1)S(1)}, bf16[64,128,4,128]{1,0,3,2:T(8,128)(2,1)}, u32[]{:S(2)}) copy-start(bf16[64,128,4,128]{1,0,3,2:T(8,128)(2,1)} %copy.24) | copy-start | bytes 25165828
  159.4 285.8 %reduce-scatter.3.cloned.1.call-start = ((), (), s32[]{:S(2)}) async-start(), calls=%async_computation.4 | async-start | bytes 5406720 | tf_op jit(solution)/shard_map/reduce_scatter | solution.py:158
  199.6 12.2 %copy-start.3 = (bf16[128,8192]{1,0:T(8,128)(2,1)S(1)}, bf16[128,8192]{1,0:T(8,128)(2,1)}, u32[]{:S(2)}) copy-start(bf16[128,8192]{1,0:T(8,128)(2,1)} %param.15) | copy-start | bytes 6291460
  211.8 12.2 %copy-start.2 = (bf16[4,128,64,128]{3,2,1,0:T(8,128)(2,1)S(1)}, bf16[4,128,64,128]{3,2,1,0:T(8,128)(2,1)}, u32[]{:S(2)}) copy-start(bf16[4,128,64,128]{3,2,1,0:T(8,128)(2,1)} %copy.22) | copy-start | bytes 25165828
Sparse Core Ops, SparseCore 0:
  10.8 68.1 all-gather.4
  81.8 63.7 all-gather.2
  159.5 142.8 reduce-scatter.4
  305.1 140.0 reduce-scatter.2
where the time goes:
time: 459 us; the launch traced here: 452 us
  waiting for transfers between devices  211 us (46%)
  local copies, waits for them, and re-layouts  120 us (26%)
  matrix products  61 us (13%)
  blocking collectives  42.2 us (9%)
  between operations  14.5 us (3%)
    reduce_scatter x1, waiting for transfers between devices, per_device(): lax.psum_scatter(terms_in.astype(jnp.bfloat16), 'dp', scatter_dimension=1...  143 us
    reduce_scatter x1, waiting for transfers between devices, per_device(): lax.psum_scatter(terms_out.astype(jnp.bfloat16), 'dp', scatter_dimension=...  52.5 us
    scatter x2, local copies, waits for them, and re-layouts, expand(): flat = flat.at[places].set(blocks, mode='drop')  48.4 us
    squeeze x1, blocking collectives, per_device(): all_in[0]  42.2 us
    transpose x2, local copies, waits for them, and re-layouts, expand(): return flat.reshape(rows_b, cols_b, BLOCK, BLOCK).transpose(0, 2, 1, 3).r...  24.5 us
    dot_general x2, matrix products, backward_layer(): pre = jnp.dot(normed, mat_a, preferred_element_type=jnp.float32)  21.4 us
    dot_general x2, matrix products, backward_layer(): lax.dot_general(upstream, mat_b, (((1,), (1,)), ((), ())), preferred_elem...  20.6 us
    dot_general x2, matrix products, slot_grads(): jnp.einsum('tjb,tjc->jbc', left_blocks, right_blocks, preferred_element_t...  19 us
  transfers between devices with their start and end apart: 4, of which 3 were waited for; matrix products, arithmetic and copies ran while one was open for 41% of the time, Pallas kernels for 0%

commit v1 on v0

--- a/solution.py
+++ b/solution.py
@@ -1,6 +1,10 @@
+import functools
+
 import jax
 import jax.numpy as jnp
 from jax import lax
+from jax.experimental import pallas as pl
+from jax.experimental.pallas import tpu as pltpu
 from jax.sharding import PartitionSpec as P
 
 D = 8192
@@ -165,6 +169,379 @@
     return (sums_in.astype(jnp.bfloat16), sums_out.astype(jnp.bfloat16))
 
 
+EXTRA= 16
+WIDE = 1024
+
+
+class Place:
+    def __init__(self, devices):
+        me = lax.axis_index("dp")
+        self.depth = devices // 8
+        self.me = me
+        self.core = me % 2
+        self.chip = me // 2
+        x = self.chip % 2
+        y = (self.chip // 2) % 2
+        self.z = self.chip // 4
+        dx = 1 - 2 * x
+        dy = 2 * (1 - 2 * y)
+        self.first = (1 - self.core) * dx + self.core * dy
+        self.second = (1 - self.core) * dy + self.core * dx
+        self.sibling = me + 1 - 2 * self.core
+
+    def member(self, ds, df, dz, first=None, second=None):
+        first = self.first if first is None else first
+        second = self.second if second is None else second
+        along = ((self.z + dz) % self.depth - self.z) * 4
+        return self.chip + along + df * first + ds * second
+
+    def device(self, ds, df, dz):
+        return 2 * self.member(ds, df, dz) + self.core
+
+    def greet(self):
+        peers = [self.sibling, self.device(1, 0, 0), self.device(0, 1, 0)]
+        peers += [self.device(0, 0, d) for d in range(1, self.depth)]
+        barrier = pltpu.get_barrier_semaphore()
+        for peer in peers:
+            pl.semaphore_signal(
+                barrier, inc=1, device_id={"dp": peer}, device_id_type=pl.DeviceIdType.MESH
+            )
+        pl.semaphore_wait(barrier, len(peers))
+
+
+def remote(src, dst, send, recv, peer):
+    return pltpu.make_async_remote_copy(
+        src_ref=src,
+        dst_ref=dst,
+        send_sem=send,
+        recv_sem=recv,
+        device_id={"dp": peer},
+        device_id_type=pl.DeviceIdType.MESH,
+    )
+
+
+def gather_kernel(devices, own, full, send_sems, chip_sems, sib_sems, pair_sems, copy_sems):
+    at = Place(devices)
+    depth = at.depth
+    mine = at.core
+    sends = []
+    pair = []
+    local = []
+    for m in range(2):
+        local.append(pltpu.make_async_copy(own.at[m], full.at[m, at.me], copy_sems.at[m]))
+        local[-1].start()
+    at.greet()
+
+    def start(src, dst, recv, peer):
+        copy = remote(src, dst, send_sems.at[len(sends)], recv, peer)
+        copy.start()
+        sends.append(copy)
+        return copy
+
+    for m in range(2):
+        pair.append(start(own.at[m], full.at[m, at.me], pair_sems.at[m], at.sibling))
+
+    def shard(chip):
+        return full.at[mine, pl.ds(2 * chip, 2)]
+
+    def push(chip, peer):
+        start(shard(chip), shard(chip), chip_sems.at[chip], peer)
+
+    def share(chip):
+        start(shard(chip), shard(chip), sib_sems.at[chip], at.sibling)
+
+    def arrived(chip):
+        remote(shard(chip), shard(chip), send_sems.at[0], chip_sems.at[chip], at.sibling).wait_recv()
+
+    first, second = at.device(0, 1, 0), at.device(1, 0, 0)
+    for copy in local:
+        copy.wait()
+    for copy in pair:
+        copy.wait_recv()
+    here = at.chip
+    order = list(range(1, depth))
+    order = sorted(order, key=lambda d: (min(d, depth - d), d))
+    push(here, second)
+    push(here, first)
+    for d in order:
+        push(here, at.device(0, 0, d))
+    for d in [0] + order:
+        if d:
+            chip = at.member(0, 0, d)
+            arrived(chip)
+            push(chip, first)
+            push(chip, second)
+            share(chip)
+        chip = at.member(0, 1, d)
+        arrived(chip)
+        push(chip, second)
+        share(chip)
+    for df in range(2):
+        for d in [0] + order:
+            chip = at.member(1, df, d)
+            arrived(chip)
+            share(chip)
+    for df in range(2):
+        for ds in range(2):
+            for d in range(depth):
+                if df or ds or d:
+                    chip = at.member(ds, df, d)
+                    other = full.at[1 - mine, pl.ds(2 * chip, 2)]
+                    remote(other, other, send_sems.at[0], sib_sems.at[chip], at.sibling).wait_recv()
+    for copy in sends:
+        copy.wait_send()
+
+
+def gather_blocks(own, devices):
+    chips = devices // 2
+    depth = devices // 8
+    sends = 2 + 2 + (depth - 1) + 3 * (depth - 1) + 2 * depth + 2 * depth
+    return pl.pallas_call(
+        functools.partial(gather_kernel, devices),
+        out_shape=jax.ShapeDtypeStruct((2, devices) + own.shape[1:], own.dtype),
+        in_specs=[pl.BlockSpec(memory_space=pltpu.VMEM)],
+        out_specs=pl.BlockSpec(memory_space=pl.ANY),
+        scratch_shapes=[
+            pltpu.SemaphoreType.DMA((sends,)),
+            pltpu.SemaphoreType.DMA((chips,)),
+            pltpu.SemaphoreType.DMA((chips,)),
+            pltpu.SemaphoreType.DMA((2,)),
+            pltpu.SemaphoreType.DMA((2,)),
+        ],
+        compiler_params=pltpu.CompilerParams(collective_id=0, has_side_effects=True),
+        name="gather_blocks",
+    )(own)
+
+
+def layer_kernel(per, pos, tokens, upper, full, out, mat_a, mat_b, normed):
+    count, width = tokens.shape
+    rank = mat_a.shape[1]
+    devices = full.shape[1]
+    rows_k = rank // BLOCK
+    rows_d = width // BLOCK
+    chunks = [slice(i, i + WIDE) for i in range(0, width, WIDE)]
+
+    def wipe_a(i, carry):
+        mat_a[pl.ds(pl.multiple_of(i * BLOCK, BLOCK), BLOCK), :] = jnp.zeros((BLOCK, rank), jnp.bfloat16)
+        return carry
+
+    lax.fori_loop(0, rows_d, wipe_a, 0)
+
+    def wipe_b(i, carry):
+        mat_b[:, pl.ds(pl.multiple_of(i * BLOCK, BLOCK), BLOCK)] = jnp.zeros(
+            (mat_b.shape[0], BLOCK), jnp.bfloat16
+        )
+        return carry
+
+    lax.fori_loop(0, rows_d, wipe_b, 0)
+
+    def spot_a(j):
+        p = pos[0, j]
+        return (
+            pl.ds(pl.multiple_of((p // rows_k) * BLOCK, BLOCK), BLOCK),
+            pl.ds(pl.multiple_of((p % rows_k) * BLOCK, BLOCK), BLOCK),
+        )
+
+    def spot_b(j):
+        p = pos[1, j]
+        return (
+            pl.ds(pl.multiple_of((p // rows_d) * BLOCK, BLOCK), BLOCK),
+            pl.ds(pl.multiple_of((p % rows_d) * BLOCK, BLOCK), BLOCK),
+        )
+
+    def place(dev, carry):
+        for i in range(per):
+            rows = pl.ds(i * BLOCK, BLOCK)
+            r, c = spot_a(dev * per + i)
+            mat_a[r, c] = full[0, dev, rows, :]
+            r, c = spot_b(dev * per + i)
+            mat_b[r, c] = full[1, dev, rows, :]
+        return carry
+
+    lax.fori_loop(0, devices, place, 0)
+
+    total = jnp.zeros((count, BLOCK), jnp.float32)
+    for k in range(0, width, BLOCK):
+        wide = tokens[:, k : k + BLOCK].astype(jnp.float32)
+        total += wide * wide
+    scale = jnp.sqrt(jnp.sum(total, axis=-1, keepdims=True) / width + EPS)
+    inverse = 1.0 / scale
+    pre = jnp.zeros((count, rank), jnp.float32)
+    dact = jnp.zeros((count, rank), jnp.float32)
+    for k in chunks:
+        unit = (tokens[:, k].astype(jnp.float32) * inverse).astype(jnp.bfloat16)
+        normed[:, k] = unit
+        pre += jnp.dot(unit, mat_a[k, :], preferred_element_type=jnp.float32)
+        dact += lax.dot_general(
+            upper[:, k], mat_b[:rank, k], (((1,), (1,)), ((), ())), preferred_element_type=jnp.float32
+        )
+    sig = jax.nn.sigmoid(pre)
+    act = (pre * sig).astype(jnp.bfloat16)
+    dpre = (dact * sig * (1.0 + pre * (1.0 - sig))).astype(jnp.bfloat16)
+    across = (((0,), (0,)), ((), ()))
+    mat_a[width:, :] = jnp.zeros((BLOCK, rank), jnp.bfloat16)
+    mat_b[rank:, :] = jnp.zeros((BLOCK, width), jnp.bfloat16)
+    for k in chunks:
+        mat_a[k, :] = lax.dot_general(
+            normed[:, k], dpre, across, preferred_element_type=jnp.float32
+        ).astype(jnp.bfloat16)
+        mat_b[:rank, k] = lax.dot_general(
+            act, upper[:, k], across, preferred_element_type=jnp.float32
+        ).astype(jnp.bfloat16)
+
+    def pick(dev, carry):
+        for i in range(per):
+            rows = pl.ds(i * BLOCK, BLOCK)
+            r, c = spot_a(dev * per + i)
+            out[0, dev, rows, :] = mat_a[r, c]
+            r, c = spot_b(dev * per + i)
+            out[1, dev, rows, :] = mat_b[r, c]
+        return carry
+
+    lax.fori_loop(0, devices, pick, 0)
+
+
+def layer_terms(places, tokens, upper, full, per):
+    count, width = tokens.shape
+    devices = full.shape[1]
+    vmem = pl.BlockSpec(memory_space=pltpu.VMEM)
+    return pl.pallas_call(
+        functools.partial(layer_kernel, per),
+        out_shape=jax.ShapeDtypeStruct((2, devices, per * BLOCK, BLOCK), jnp.bfloat16),
+        in_specs=[pl.BlockSpec(memory_space=pltpu.SMEM), vmem, vmem, vmem],
+        out_specs=vmem,
+        scratch_shapes=[
+            pltpu.VMEM((width + BLOCK, RANK), jnp.bfloat16),
+            pltpu.VMEM((RANK + BLOCK, width), jnp.bfloat16),
+            pltpu.VMEM((count, width), jnp.bfloat16),
+        ],
+        compiler_params=pltpu.CompilerParams(vmem_limit_bytes=60 * 1024 * 1024),
+        name="layer_terms",
+    )(places, tokens, upper, full)
+
+
+def scatter_kernel(devices, terms, out, held, final, pair_got, second_got, first_got, line_got, last_got,
+                   load_sems, send_sems, pair_sems, second_sems, first_sems, line_sems, last_sem):
+    at = Place(devices)
+    depth = at.depth
+    mine = at.core
+    sends = []
+    line = [0] + sorted(range(1, depth), key=lambda d: (min(d, depth - d), d))
+    far = line[1:][::-1]
+    order = [(1, 1, d) for d in far + [0]] + [(1, 0, d) for d in far + [0]]
+    order += [(0, 1, d) for d in far + [0]] + [(0, 0, d) for d in far + [0]]
+    loads = []
+    for i, (ds, df, dz) in enumerate(order):
+        chip = at.member(ds, df, dz)
+        load = pltpu.make_async_copy(terms.at[mine, pl.ds(2 * chip, 2)], held.at[i], load_sems.at[i])
+        load.start()
+        loads.append(load)
+    at.greet()
+
+    def start(src, dst, recv, peer):
+        copy = remote(src, dst, send_sems.at[len(sends)], recv, peer)
+        copy.start()
+        sends.append(copy)
+        return copy
+
+    pairs = []
+    for i, (ds, df, dz) in enumerate(order):
+        chip = at.member(ds, df, dz, at.second, at.first)
+        pairs.append(
+            start(terms.at[1 - mine, pl.ds(2 * chip, 2)], pair_got.at[i], pair_sems.at[i], at.sibling)
+        )
+
+    def got(buf, sem):
+        remote(buf, buf, send_sems.at[0], sem, at.sibling).wait_recv()
+
+    for i, (ds, df, dz) in enumerate(order):
+        loads[i].wait()
+        parts = [pair_got.at[i]]
+        pairs[i].wait_recv()
+        if not ds:
+            parts.append(second_got.at[df * depth + dz])
+            got(parts[-1], second_sems.at[df * depth + dz])
+        if not ds and not df:
+            parts.append(first_got.at[dz])
+            got(parts[-1], first_sems.at[dz])
+            if not dz:
+                for d in range(1, depth):
+                    parts.append(line_got.at[d - 1])
+                    got(parts[-1], line_sems.at[d - 1])
+        rows = held.shape[2]
+
+        def add(step, carry, i=i, parts=parts):
+            part = pl.ds(pl.multiple_of(step * BLOCK, BLOCK), BLOCK)
+            for half in range(2):
+                value = held[i, half, part, :].astype(jnp.float32)
+                for p in parts:
+                    value += p[half, part, :].astype(jnp.float32)
+                held[i, half, part, :] = value.astype(jnp.bfloat16)
+            return carry
+
+        lax.fori_loop(0, rows // BLOCK, add, 0)
+        if ds:
+            start(held.at[i], second_got.at[df * depth + dz], second_sems.at[df * depth + dz], at.device(1, 0, 0))
+        elif df:
+            start(held.at[i], first_got.at[dz], first_sems.at[dz], at.device(0, 1, 0))
+        elif dz:
+            start(held.at[i], line_got.at[dz - 1], line_sems.at[dz - 1], at.device(0, 0, dz))
+        else:
+            last = start(held.at[i, 1 - mine], last_got, last_sem, at.sibling)
+            final[...] = held[i, mine]
+            last.wait_recv()
+    out[mine] = final[...]
+    out[1 - mine] = last_got[...]
+    for copy in sends:
+        copy.wait_send()
+
+
+def scatter_terms(terms, devices):
+    chips = devices // 2
+    depth = devices // 8
+    rows = terms.shape[2]
+    shard = (2, rows, BLOCK)
+    dma = pltpu.SemaphoreType.DMA
+    return pl.pallas_call(
+        functools.partial(scatter_kernel, devices),
+        out_shape=jax.ShapeDtypeStruct(shard, jnp.bfloat16),
+        in_specs=[pl.BlockSpec(memory_space=pl.ANY)],
+        out_specs=pl.BlockSpec(memory_space=pltpu.VMEM),
+        scratch_shapes=[
+            pltpu.VMEM((chips,) + shard, jnp.bfloat16),
+            pltpu.VMEM((rows, BLOCK), jnp.bfloat16),
+            pltpu.VMEM((chips,) + shard, jnp.bfloat16),
+            pltpu.VMEM((2 * depth,) + shard, jnp.bfloat16),
+            pltpu.VMEM((depth,) + shard, jnp.bfloat16),
+            pltpu.VMEM((depth - 1,) + shard, jnp.bfloat16),
+            pltpu.VMEM((rows, BLOCK), jnp.bfloat16),
+            dma((chips,)),
+            dma((2 * chips,)),
+            dma((chips,)),
+            dma((2 * depth,)),
+            dma((depth,)),
+            dma((depth - 1,)),
+            dma,
+        ],
+        compiler_params=pltpu.CompilerParams(collective_id=1, has_side_effects=True),
+        name="scatter_terms",
+    )(terms)
+
+
+def one_section(tokens, blocks_in, blocks_out, pos_in, pos_out, cotangent):
+    devices = lax.axis_size("dp")
+    per = blocks_in.shape[1]
+    blocks = jnp.stack([blocks_in[0], blocks_out[0]]).reshape(2, per * BLOCK, BLOCK)
+    places = jnp.concatenate([pos_in, pos_out]).astype(jnp.bfloat16)
+    places = jnp.pad(places[:, None, :], ((0, 0), (0, EXTRA - 1), (0, BLOCK - per)))
+    full = gather_blocks(jnp.concatenate([blocks, places], axis=1), devices)
+    everywhere = full[:, :, per * BLOCK, :per].astype(jnp.int32).reshape(2, devices * per)
+    terms = layer_terms(everywhere, tokens, cotangent, full, per)
+    sums = scatter_terms(terms, devices)
+    shape = blocks_in.shape
+    return (sums[0].reshape(shape), sums[1].reshape(shape))
+
+
 def solution(mesh):
     in_specs = (
         P("dp", None),
@@ -175,6 +552,7 @@
         P("dp", None),
     )
     out_specs = (P("section", "dp", None, None), P("section", "dp", None, None))
+    body = one_section if mesh.shape["section"] == 1 else per_device
     return jax.shard_map(
-        per_device, mesh=mesh, in_specs=in_specs, out_specs=out_specs, check_vma=False
-    )
+        body, mesh=mesh, in_specs=in_specs, out_specs=out_specs, check_vma=False
+    )

time: 459 us -> 166 us (0.36); the launches traced: 452 us -> 165 us
  waiting for transfers between devices: 211 us -> 0 us
  Pallas kernels: 0 us -> 159 us
  local copies, waits for them, and re-layouts: 120 us -> 2.42 us
  matrix products: 61 us -> 0 us
  blocking collectives: 42.2 us -> 0 us
  between operations: 14.5 us -> 0.65 us
    reduce_scatter x2 -> x0, waiting for transfers between devices: 195 us -> none  [the longest x1 143 us: per_device(): lax.psum_scatter(terms_in.astype(jnp.bfloat16), 'dp', scatter_dimension=1...]
    pallas_call x0 -> x3, Pallas kernels: none -> 159 us  [the longest x1 65.6 us: scatter_terms(): pl.pallas_call(functools.partial(scatter_kernel, devices), out_shape=jax....]
    dot_general x6 -> x0, matrix products: 61 us -> none  [the longest x2 21.4 us: backward_layer(): pre = jnp.dot(normed, mat_a, preferred_element_type=jnp.float32)]
    scatter x2 -> x0, local copies, waits for them, and re-layouts: 48.4 us -> none  [expand(): flat = flat.at[places].set(blocks, mode='drop')]
    squeeze x1 -> x0, blocking collectives: 42.2 us -> none  [per_device(): all_in[0]]
    gather x4 -> x0, local copies, waits for them, and re-layouts: 31 us -> none  [the longest x2 15.6 us: slot_grads(): jnp.take(right.reshape(count, cols_b, BLOCK), col_block, axis=1)]
    transpose x2 -> x0, local copies, waits for them, and re-layouts: 24.5 us -> none  [expand(): return flat.reshape(rows_b, cols_b, BLOCK, BLOCK).transpose(0, 2, 1, 3).r...]
    all_gather x2 -> x0, waiting for transfers between devices: 14.1 us -> none  [the longest x1 14.1 us: per_device(): lax.all_gather(blocks_in, 'dp', axis=1, tiled=True)]
  transfers between devices with their start and end apart: 4 -> 0, of which waited for: 3 -> 0; matrix products, arithmetic and copies ran while one was open for 41% -> 0% of each run, Pallas kernels for 0% -> 0%
where the time goes in v1:
time: 166 us; the launch traced here: 165 us
  Pallas kernels  159 us (96%)
  other arithmetic  3.48 us (2%)
  local copies, waits for them, and re-layouts  2.42 us (1%)
    pallas_call x1, Pallas kernels, scatter_terms(): pl.pallas_call(functools.partial(scatter_kernel, devices), out_shape=jax....  65.6 us
    pallas_call x1, Pallas kernels, gather_blocks(): pl.pallas_call(functools.partial(gather_kernel, devices), out_shape=jax.S...  63.6 us
    pallas_call x1, Pallas kernels, layer_terms(): pl.pallas_call(functools.partial(layer_kernel, per), out_shape=jax.ShapeD...  29.3 us

profile of v1, /device:TPU:0, one launch (start us, length us, event | category | flops | bytes accessed | tf_op | source)
XLA Modules:
  0.0 165.1 jit_solution(12684788371452606486)
XLA Ops:
  0.6 0.7 convert_bitcast_fusion
  1.3 1.0 pad_maximum_fusion.1
  2.3 0.8 pad_maximum_fusion.own
  3.1 63.6 %gather_blocks.1.full = bf16[2,32,656,128]{3,2,1,0:T(8,128)(2,1)} custom-call(bf16[2,656,128]{2,1,0:T(8,128)(2,1)} %pad_maximum_fusion.own), custom_call_target="tpu_custom_call" | custom-call | tf_op jit(solution)/shard_map/gather_blocks/pallas_call | solution.py:299
  66.7 1.0 convert_reduce_fusion
  67.7 0.7 reshape.43.pos
  68.4 29.3 %layer_terms.1.terms = bf16[2,32,640,128]{3,2,1,0:T(8,128)(2,1)} custom-call(s32[2,160]{1,0:T(2,128)} %reshape.43.pos, bf16[128,8192]{1,0:T(8,128)(2,1)} %tokens.1, bf16[128,8192]{1,0:T(8,128)(2,1)} %upper.1, bf16[2,32,656,128]{3,2,1,0:T(8,128)(2,1)} %gather_blocks.1.full), custom_call_target="tpu_custom_call" | custom-call | tf_op jit(solution)/shard_map/layer_terms/pallas_call | solution.py:408
  97.7 65.6 %scatter_terms.1 = bf16[2,640,128]{2,1,0:T(8,128)(2,1)} custom-call(bf16[2,32,640,128]{3,2,1,0:T(8,128)(2,1)} %layer_terms.1.terms), custom_call_target="tpu_custom_call" | custom-call | tf_op jit(solution)/shard_map/scatter_terms/pallas_call | solution.py:505
  163.4 1.7 %fusion.6 = (bf16[1,640,128]{2,1,0:T(8,128)(2,1)}, bf16[1,640,128]{2,1,0:T(8,128)(2,1)}) fusion(bf16[2,640,128]{2,1,0:T(8,128)(2,1)} %scatter_terms.1), kind=kLoop, calls=%fused_computation.13 | loop fusion | bytes 655360 | tf_op jit(solution)/shard_map/slice | solution.py:542
  (1 shorter events, 0.0 us)

commit v2 on v0

--- a/solution.py
+++ b/solution.py
@@ -1,6 +1,10 @@
+import functools
+
 import jax
 import jax.numpy as jnp
 from jax import lax
+from jax.experimental import pallas as pl
+from jax.experimental.pallas import tpu as pltpu
 from jax.sharding import PartitionSpec as P
 
 D = 8192
@@ -165,6 +169,387 @@
     return (sums_in.astype(jnp.bfloat16), sums_out.astype(jnp.bfloat16))
 
 
+EXTRA= 16
+WIDE = 1024
+
+
+class Place:
+    def __init__(self, devices):
+        me = lax.axis_index("dp")
+        self.depth = devices // 8
+        self.me = me
+        self.core = me % 2
+        self.chip = me // 2
+        x = self.chip % 2
+        y = (self.chip // 2) % 2
+        self.z = self.chip // 4
+        dx = 1 - 2 * x
+        dy = 2 * (1 - 2 * y)
+        self.first = (1 - self.core) * dx + self.core * dy
+        self.second = (1 - self.core) * dy + self.core * dx
+        self.sibling = me + 1 - 2 * self.core
+
+    def member(self, ds, df, dz, first=None, second=None):
+        first = self.first if first is None else first
+        second = self.second if second is None else second
+        along = ((self.z + dz) % self.depth - self.z) * 4
+        return self.chip + along + df * first + ds * second
+
+    def device(self, ds, df, dz):
+        return 2 * self.member(ds, df, dz) + self.core
+
+    def knock(self):
+        peers = [self.sibling, self.device(1, 0, 0), self.device(0, 1, 0)]
+        peers += [self.device(0, 0, d) for d in range(1, self.depth)]
+        barrier = pltpu.get_barrier_semaphore()
+        for peer in peers:
+            pl.semaphore_signal(
+                barrier, inc=1, device_id={"dp": peer}, device_id_type=pl.DeviceIdType.MESH
+            )
+        return lambda: pl.semaphore_wait(barrier, len(peers))
+
+
+def remote(src, dst, send, recv, peer):
+    return pltpu.make_async_remote_copy(
+        src_ref=src,
+        dst_ref=dst,
+        send_sem=send,
+        recv_sem=recv,
+        device_id={"dp": peer},
+        device_id_type=pl.DeviceIdType.MESH,
+    )
+
+
+def gather_kernel(devices, own, own_tags, tokens, cotangent, full, tags, other, send_sems, chip_sems, misc_sems):
+    at = Place(devices)
+    depth = at.depth
+    mine = at.core
+    sends = []
+    local = [
+        pltpu.make_async_copy(own.at[mine], full.at[at.me], misc_sems.at[0]),
+        pltpu.make_async_copy(own_tags.at[mine], tags.at[at.me], misc_sems.at[3]),
+    ]
+    for copy in local:
+        copy.start()
+    at.knock()()
+
+    def start(src, dst, recv, peer):
+        copy = remote(src, dst, send_sems.at[len(sends)], recv, peer)
+        copy.start()
+        sends.append(copy)
+        return copy
+
+    pair = [
+        start(own.at[1 - mine], full.at[at.me], misc_sems.at[1], at.sibling),
+        start(own_tags.at[1 - mine], tags.at[at.me], misc_sems.at[4], at.sibling),
+    ]
+
+    def shards(chip):
+        return ((full.at[pl.ds(2 * chip, 2)], chip_sems.at[0, chip]), (tags.at[pl.ds(2 * chip, 2)], chip_sems.at[1, chip]))
+
+    def push(chip, peer):
+        for shard, sem in shards(chip):
+            start(shard, shard, sem, peer)
+
+    def arrived(chip):
+        for shard, sem in shards(chip):
+            remote(shard, shard, send_sems.at[0], sem, at.sibling).wait_recv()
+
+    first, second = at.device(0, 1, 0), at.device(1, 0, 0)
+    for copy in local:
+        copy.wait()
+    for copy in pair:
+        copy.wait_recv()
+    here = at.chip
+    order = list(range(1, depth))
+    order = sorted(order, key=lambda d: (min(d, depth - d), d))
+    push(here, second)
+    push(here, first)
+    for d in order:
+        push(here, at.device(0, 0, d))
+    give = remote(tokens, other, send_sems.at[len(sends)], misc_sems.at[2], at.sibling)
+
+    @pl.when(mine == 0)
+    def _():
+        remote(cotangent, other, send_sems.at[len(sends)], misc_sems.at[2], at.sibling).start()
+
+    @pl.when(mine == 1)
+    def _():
+        give.start()
+
+    sends.append(give)
+    for d in [0] + order:
+        if d:
+            chip = at.member(0, 0, d)
+            arrived(chip)
+            push(chip, first)
+            push(chip, second)
+        chip = at.member(0, 1, d)
+        arrived(chip)
+        push(chip, second)
+    for df in range(2):
+        for d in [0] + order:
+            arrived(at.member(1, df, d))
+    give.wait_recv()
+    for copy in sends:
+        copy.wait_send()
+
+
+def gather_blocks(own, own_tags, tokens, cotangent, devices):
+    chips = devices // 2
+    depth = devices // 8
+    sends = 2 * (1 + 2 + (depth - 1) + 2 * (depth - 1) + depth) + 1
+    anywhere = pl.BlockSpec(memory_space=pl.ANY)
+    return pl.pallas_call(
+        functools.partial(gather_kernel, devices),
+        out_shape=(
+            jax.ShapeDtypeStruct((devices,) + own.shape[1:], own.dtype),
+            jax.ShapeDtypeStruct((devices,) + own_tags.shape[1:], own_tags.dtype),
+            jax.ShapeDtypeStruct(tokens.shape, tokens.dtype),
+        ),
+        in_specs=[pl.BlockSpec(memory_space=pltpu.VMEM)] * 2 + [anywhere, anywhere],
+        out_specs=(anywhere, anywhere, anywhere),
+        scratch_shapes=[
+            pltpu.SemaphoreType.DMA((sends,)),
+            pltpu.SemaphoreType.DMA((2, chips)),
+            pltpu.SemaphoreType.DMA((5,)),
+        ],
+        compiler_params=pltpu.CompilerParams(collective_id=0, has_side_effects=True),
+        name="gather_blocks",
+    )(own, own_tags, tokens, cotangent)
+
+
+def layer_kernel(devices, per, pos, begin, tokens, cotangent, other, full, out,
+                 blocks, rows, mat_a, mat_b, grads, middle, middle_got, inverse,
+                 held, second_got, first_got, line_got, last_got,
+                 load_sems, send_sems, second_sems, first_sems, line_sems, pair_sems):
+    at = Place(devices)
+    depth = at.depth
+    mine = at.core
+    count, width = tokens.shape
+    rank = mat_a.shape[1]
+    rows_k = rank // BLOCK
+    rows_d = width // BLOCK
+    chunks = [slice(i, i + WIDE) for i in range(0, width, WIDE)]
+    sends = []
+
+    def start(src, dst, recv, peer):
+        copy = remote(src, dst, send_sems.at[len(sends)], recv, peer)
+        copy.start()
+        sends.append(copy)
+        return copy
+
+    def got(buf, sem):
+        remote(buf, buf, send_sems.at[0], sem, at.sibling).wait_recv()
+
+    used = full.shape[0]
+    load_blocks = pltpu.make_async_copy(full, blocks.at[pl.ds(0, used)], load_sems.at[0])
+    load_blocks.start()
+    load_own = pltpu.make_async_copy(tokens, rows.at[pl.ds(mine * count, count)], load_sems.at[1])
+
+    @pl.when(mine == 0)
+    def _():
+        load_own.start()
+
+    @pl.when(mine == 1)
+    def _():
+        pltpu.make_async_copy(cotangent, rows.at[pl.ds(mine * count, count)], load_sems.at[1]).start()
+
+    load_other = pltpu.make_async_copy(other, rows.at[pl.ds((1 - mine) * count, count)], load_sems.at[2])
+    load_other.start()
+    wait_peers = at.knock()
+    blocks[used] = jnp.zeros((BLOCK, BLOCK), jnp.bfloat16)
+    grads[rows_d * rows_k] = jnp.zeros((BLOCK, BLOCK), jnp.bfloat16)
+    load_blocks.wait()
+
+    def slot_of(b):
+        return blocks[begin[b]]
+
+    @pl.when(mine == 0)
+    def _():
+        def expand_a(r, carry):
+            into = pl.ds(pl.multiple_of(r * BLOCK, BLOCK), BLOCK)
+            for c in range(rows_k):
+                mat_a[into, c * BLOCK : (c + 1) * BLOCK] = slot_of(r * rows_k + c)
+            return carry
+
+        lax.fori_loop(0, rows_d, expand_a, 0)
+
+    @pl.when(mine == 1)
+    def _():
+        def expand_b(c, carry):
+            into = pl.ds(pl.multiple_of(c * BLOCK, BLOCK), BLOCK)
+            for r in range(rows_k):
+                mat_b[r * BLOCK : (r + 1) * BLOCK, into] = slot_of(r * rows_d + c)
+            return carry
+
+        lax.fori_loop(0, rows_d, expand_b, 0)
+
+    load_own.wait()
+    load_other.wait()
+
+    @pl.when(mine == 0)
+    def _():
+        total = jnp.zeros((2 * count, BLOCK), jnp.float32)
+        for k in range(0, width, BLOCK):
+            wide = rows[:, k : k + BLOCK].astype(jnp.float32)
+            total += wide * wide
+        scale = jnp.sqrt(jnp.sum(total, axis=-1, keepdims=True) / width + EPS)
+        inverse[...] = jnp.broadcast_to(1.0 / scale, inverse.shape)
+        pre = jnp.zeros((2 * count, rank), jnp.float32)
+        for k in chunks:
+            pre += jnp.dot(rows[:, k], mat_a[k, :], preferred_element_type=jnp.float32)
+        middle[...] = pre * inverse[:, :1]
+
+    @pl.when(mine == 1)
+    def _():
+        dact = jnp.zeros((2 * count, rank), jnp.float32)
+        for k in chunks:
+            dact += lax.dot_general(
+                rows[:, k], mat_b[:, k], (((1,), (1,)), ((), ())), preferred_element_type=jnp.float32
+            )
+        middle[...] = dact
+
+    wait_peers()
+    start(middle, middle_got, pair_sems.at[0], at.sibling).wait_recv()
+    across = (((0,), (0,)), ((), ()))
+
+    @pl.when(mine == 0)
+    def _():
+        pre = middle[...]
+        sig = jax.nn.sigmoid(pre)
+        dpre = middle_got[...] * sig * (1.0 + pre * (1.0 - sig))
+        dpre = (dpre * inverse[:, :1]).astype(jnp.bfloat16)
+        for k in chunks:
+            part = lax.dot_general(
+                rows[:, k], dpre, across, preferred_element_type=jnp.float32
+            ).astype(jnp.bfloat16)
+            for r in range(WIDE // BLOCK):
+                for c in range(rows_k):
+                    grads[(k.start // BLOCK + r) * rows_k + c] = part[
+                        r * BLOCK : (r + 1) * BLOCK, c * BLOCK : (c + 1) * BLOCK
+                    ]
+
+    @pl.when(mine == 1)
+    def _():
+        pre = middle_got[...]
+        act = (pre * jax.nn.sigmoid(pre)).astype(jnp.bfloat16)
+        for k in chunks:
+            part = lax.dot_general(
+                act, rows[:, k], across, preferred_element_type=jnp.float32
+            ).astype(jnp.bfloat16)
+            for r in range(rows_k):
+                for c in range(WIDE // BLOCK):
+                    grads[r * rows_d + k.start // BLOCK + c] = part[
+                        r * BLOCK : (r + 1) * BLOCK, c * BLOCK : (c + 1) * BLOCK
+                    ]
+
+    line = sorted(range(1, depth), key=lambda d: (min(d, depth - d), d))
+    dist = line[::-1] + [0]
+    order = [(ds, df, d) for ds, df in ((1, 1), (1, 0), (0, 1), (0, 0)) for d in dist]
+    for i, (ds, df, dz) in enumerate(order):
+        chip = at.member(ds, df, dz)
+        parts = []
+        if not ds:
+            parts.append(second_got.at[df * depth + dz])
+            got(parts[-1], second_sems.at[df * depth + dz])
+        if not ds and not df:
+            parts.append(first_got.at[dz])
+            got(parts[-1], first_sems.at[dz])
+            if not dz:
+                for d in range(1, depth):
+                    parts.append(line_got.at[d - 1])
+                    got(parts[-1], line_sems.at[d - 1])
+
+        def fill(step, carry, i=i, parts=parts, chip=chip):
+            half = step // per
+            part = pl.ds(pl.multiple_of((step % per) * BLOCK, BLOCK), BLOCK)
+            value = grads[pos[chip * (2 * per) + step]]
+            if parts:
+                value = value.astype(jnp.float32)
+                for q in parts:
+                    value += q[half, part, :].astype(jnp.float32)
+            held[i, half, part, :] = value.astype(jnp.bfloat16)
+            return carry
+
+        lax.fori_loop(0, 2 * per, fill, 0)
+        if ds:
+            start(held.at[i], second_got.at[df * depth + dz], second_sems.at[df * depth + dz], at.device(1, 0, 0))
+        elif df:
+            start(held.at[i], first_got.at[dz], first_sems.at[dz], at.device(0, 1, 0))
+        elif dz:
+            start(held.at[i], line_got.at[dz - 1], line_sems.at[dz - 1], at.device(0, 0, dz))
+        else:
+            last = start(held.at[i, 1 - mine], last_got, pair_sems.at[1], at.sibling)
+            out[mine] = held[i, mine]
+            last.wait_recv()
+    out[1 - mine] = last_got[...]
+    for copy in sends:
+        copy.wait_send()
+
+
+def layer_sums(places, begin, tokens, cotangent, other, full, devices, per):
+    count, width = tokens.shape
+    chips = devices // 2
+    depth = devices // 8
+    shard = (2, per * BLOCK, BLOCK)
+    dma = pltpu.SemaphoreType.DMA
+    vmem = pltpu.VMEM
+    anywhere = pl.BlockSpec(memory_space=pl.ANY)
+    scalars = pl.BlockSpec(memory_space=pltpu.SMEM)
+    bf16, f32 = jnp.bfloat16, jnp.float32
+    return pl.pallas_call(
+        functools.partial(layer_kernel, devices, per),
+        out_shape=jax.ShapeDtypeStruct(shard, bf16),
+        in_specs=[scalars, scalars, anywhere, anywhere, anywhere, anywhere],
+        out_specs=pl.BlockSpec(memory_space=vmem),
+        scratch_shapes=[
+            vmem((full.shape[0] + 1, BLOCK, BLOCK), bf16),
+            vmem((2 * count, width), bf16),
+            vmem((width, RANK), bf16),
+            vmem((RANK, width), bf16),
+            vmem((width * RANK // (BLOCK * BLOCK) + 1, BLOCK, BLOCK), bf16),
+            vmem((2 * count, RANK), f32),
+            vmem((2 * count, RANK), f32),
+            vmem((2 * count, BLOCK), f32),
+            vmem((chips,) + shard, bf16),
+            vmem((2 * depth,) + shard, bf16),
+            vmem((depth,) + shard, bf16),
+            vmem((depth - 1,) + shard, bf16),
+            vmem(shard[1:], bf16),
+            dma((3,)),
+            dma((chips + 1,)),
+            dma((2 * depth,)),
+            dma((depth,)),
+            dma((depth - 1,)),
+            dma((2,)),
+        ],
+        compiler_params=pltpu.CompilerParams(
+            collective_id=1, has_side_effects=True, vmem_limit_bytes=60 * 1024 * 1024
+        ),
+        name="layer_sums",
+    )(places, begin, tokens, cotangent, other, full)
+
+
+def one_section(tokens, blocks_in, blocks_out, pos_in, pos_out, cotangent):
+    devices = lax.axis_size("dp")
+    per = blocks_in.shape[1]
+    own = jnp.stack([blocks_in[0], blocks_out[0]])
+    places = jnp.concatenate([pos_in, pos_out]).astype(jnp.bfloat16)
+    places = jnp.pad(places[:, None, :], ((0, 0), (0, EXTRA - 1), (0, BLOCK - per)))
+    full, tags, other = gather_blocks(own, places, tokens, cotangent, devices)
+    count = devices * per
+    slots = tags[:, 0, :per].astype(jnp.int32)
+    starts = per * jnp.arange(devices)[:, None] + jnp.arange(per)[None, :]
+    numbers = jnp.arange((tokens.shape[1] // BLOCK) * (RANK // BLOCK))
+    found = jnp.where(slots[None] == numbers[:, None, None], starts[None], count)
+    begin = jnp.min(found, axis=(1, 2)).astype(jnp.int32)
+    flat = full.reshape(count, BLOCK, BLOCK)
+    sums = layer_sums(slots.reshape(-1), begin, tokens, cotangent, other, flat, devices, per)
+    shape = blocks_in.shape
+    return (sums[0].reshape(shape), sums[1].reshape(shape))
+
+
 def solution(mesh):
     in_specs = (
         P("dp", None),
@@ -175,6 +560,7 @@
         P("dp", None),
     )
     out_specs = (P("section", "dp", None, None), P("section", "dp", None, None))
+    body = one_section if mesh.shape["section"] == 1 else per_device
     return jax.shard_map(
-        per_device, mesh=mesh, in_specs=in_specs, out_specs=out_specs, check_vma=False
-    )
+        body, mesh=mesh, in_specs=in_specs, out_specs=out_specs, check_vma=False
+    )

time: 459 us -> 146 us (0.32)
  waiting for transfers between devices: 211 us -> 0 us
  Pallas kernels: 0 us -> 135 us
  local copies, waits for them, and re-layouts: 120 us -> 2.48 us
  matrix products: 61 us -> 0 us
  blocking collectives: 42.2 us -> 0 us
  between operations: 14.5 us -> 0.66 us
    reduce_scatter x2 -> x0, waiting for transfers between devices: 195 us -> none  [the longest x1 143 us: per_device(): lax.psum_scatter(terms_in.astype(jnp.bfloat16), 'dp', scatter_dimension=1...]
    pallas_call x0 -> x2, Pallas kernels: none -> 135 us  [the longest x1 73 us: layer_sums(): pl.pallas_call(functools.partial(layer_kernel, devices, per), out_shape=j...]
    dot_general x6 -> x0, matrix products: 61 us -> none  [the longest x2 21.4 us: backward_layer(): pre = jnp.dot(normed, mat_a, preferred_element_type=jnp.float32)]
    scatter x2 -> x0, local copies, waits for them, and re-layouts: 48.4 us -> none  [expand(): flat = flat.at[places].set(blocks, mode='drop')]
    squeeze x1 -> x0, blocking collectives: 42.2 us -> none  [per_device(): all_in[0]]
    gather x4 -> x0, local copies, waits for them, and re-layouts: 31 us -> none  [the longest x2 15.6 us: slot_grads(): jnp.take(right.reshape(count, cols_b, BLOCK), col_block, axis=1)]
    transpose x2 -> x0, local copies, waits for them, and re-layouts: 24.5 us -> none  [expand(): return flat.reshape(rows_b, cols_b, BLOCK, BLOCK).transpose(0, 2, 1, 3).r...]
    all_gather x2 -> x0, waiting for transfers between devices: 14.1 us -> none  [the longest x1 14.1 us: per_device(): lax.all_gather(blocks_in, 'dp', axis=1, tiled=True)]
  transfers between devices with their start and end apart: 4 -> 0, of which waited for: 3 -> 0; matrix products, arithmetic and copies ran while one was open for 41% -> 0% of each run, Pallas kernels for 0% -> 0%
where the time goes in v2:
time: 146 us; the launch traced here: 143 us
  Pallas kernels  135 us (92%)
  other arithmetic  5.48 us (4%)
  local copies, waits for them, and re-layouts  2.48 us (2%)
    pallas_call x1, Pallas kernels, layer_sums(): pl.pallas_call(functools.partial(layer_kernel, devices, per), out_shape=j...  73 us
    pallas_call x1, Pallas kernels, gather_blocks(): pl.pallas_call(functools.partial(gather_kernel, devices), out_shape=(jax....  61.5 us

profile of v2, /device:TPU:0, one launch (start us, length us, event | category | flops | bytes accessed | tf_op | source)
XLA Modules:
  0.0 143.2 jit_solution(16031805288266782618)
XLA Ops:
  0.6 0.7 convert_bitcast_fusion
  1.3 0.6 fusion.5.own_tags
  1.9 1.7 %pad_maximum_fusion.own = bf16[2,5,128,128]{3,2,1,0:T(8,128)(2,1)} fusion(bf16[1,5,128,128]{3,2,1,0:T(8,128)(2,1)} %param.8, bf16[1,5,128,128]{3,2,1,0:T(8,128)(2,1)} %param.7), kind=kLoop, calls=%fused_computation | loop fusion | flops 163840 | bytes 655360 | tf_op jit(solution)/shard_map/stack | solution.py:537
  3.7 61.5 %gather_blocks.1 = (bf16[32,5,128,128]{3,2,1,0:T(8,128)(2,1)}, bf16[32,16,128]{2,1,0:T(8,128)(2,1)}, bf16[128,8192]{1,0:T(8,128)(2,1)}) custom-call(bf16[2,5,128,128]{3,2,1,0:T(8,128)(2,1)} %pad_maximum_fusion.own, bf16[2,16,128]{2,1,0:T(8,128)(2,1)} %fusion.5.own_tags, bf16[128,8192]{1,0:T(8,128)(2,1)} %tokens.3, bf16[128,8192]{1,0:T(8,128)(2,1)} %cotangent.3), custom_call_target="tpu_custom_call" | custom-call | tf_op jit(solution)/shard_map/gather_blocks/pallas_call | solution.py:303
  65.2 0.9 slice_convert_fusion
  66.1 0.1 copy.8
  66.1 0.7 select_reduce_fusion.begin
  66.8 0.9 fusion.6
  67.7 0.7 reshape.74.pos
  68.4 73.0 %layer_sums.1 = bf16[2,640,128]{2,1,0:T(8,128)(2,1)} custom-call(s32[160]{0:T(256)} %reshape.74.pos, s32[256]{0:T(256)} %select_reduce_fusion.begin, bf16[128,8192]{1,0:T(8,128)(2,1)} %tokens.3, bf16[128,8192]{1,0:T(8,128)(2,1)} %cotangent.3, bf16[128,8192]{1,0:T(8,128)(2,1)} %get-tuple-element.6.other, bf16[160,128,128]{2,1,0:T(8,128)(2,1)} %bitcast.8), custom_call_target="tpu_custom_call" | custom-call | tf_op jit(solution)/shard_map/layer_sums/pallas_call | solution.py:501
  141.5 1.7 %fusion.7 = (bf16[1,640,128]{2,1,0:T(8,128)(2,1)}, bf16[1,640,128]{2,1,0:T(8,128)(2,1)}) fusion(bf16[2,640,128]{2,1,0:T(8,128)(2,1)} %layer_sums.1), kind=kLoop, calls=%fused_computation.17 | loop fusion | bytes 655360 | tf_op jit(solution)/shard_map/slice | solution.py:550
  (2 shorter events, 0.0 us)

commit v3 on v2

--- a/solution.py
+++ b/solution.py
@@ -220,94 +220,135 @@
     )
 
 
-def gather_kernel(devices, own, own_tags, tokens, cotangent, full, tags, other, send_sems, chip_sems, misc_sems):
+def gather_kernel(
+    devices, own_in, own_out, own_tags, tokens, cotangent, full, tags, other, send_sems, chip_sems, misc_sems
+):
     at = Place(devices)
     depth = at.depth
     mine = at.core
     sends = []
+
+    def on_core(core):
+        return pl.when(mine == core)
+
+    def local_copy(source):
+        return pltpu.make_async_copy(source, full.at[at.me], misc_sems.at[0])
+
+    on_core(0)(lambda: local_copy(own_in).start())
+    on_core(1)(lambda: local_copy(own_out).start())
     local = [
-        pltpu.make_async_copy(own.at[mine], full.at[at.me], misc_sems.at[0]),
+        local_copy(own_in),
         pltpu.make_async_copy(own_tags.at[mine], tags.at[at.me], misc_sems.at[3]),
     ]
-    for copy in local:
-        copy.start()
+    local[1].start()
     at.knock()()
 
-    def start(src, dst, recv, peer):
-        copy = remote(src, dst, send_sems.at[len(sends)], recv, peer)
-        copy.start()
-        sends.append(copy)
-        return copy
-
+    def start(src, dst, recv, peer, like, present=None):
+        remote(src, dst, send_sems.at[len(sends)], recv, peer).start()
+        sends.append((like, present))
+
+    def pair_copy(source):
+        return remote(source, full.at[at.me], send_sems.at[0], misc_sems.at[1], at.sibling)
+
+    on_core(0)(lambda: pair_copy(own_out).start())
+    on_core(1)(lambda: pair_copy(own_in).start())
+    sends.append((own_in, None))
+    start(own_tags.at[1 - mine], tags.at[at.me], misc_sems.at[4], at.sibling, own_tags.at[0])
     pair = [
-        start(own.at[1 - mine], full.at[at.me], misc_sems.at[1], at.sibling),
-        start(own_tags.at[1 - mine], tags.at[at.me], misc_sems.at[4], at.sibling),
+        pair_copy(own_in),
+        remote(own_tags.at[0], tags.at[at.me], send_sems.at[0], misc_sems.at[4], at.sibling),
     ]
 
     def shards(chip):
-        return ((full.at[pl.ds(2 * chip, 2)], chip_sems.at[0, chip]), (tags.at[pl.ds(2 * chip, 2)], chip_sems.at[1, chip]))
-
-    def push(chip, peer):
-        for shard, sem in shards(chip):
-            start(shard, shard, sem, peer)
+        return (
+            (full.at[pl.ds(2 * chip, 2)], chip_sems.at[0, chip]),
+            (tags.at[pl.ds(2 * chip, 2)], chip_sems.at[1, chip]),
+        )
+
+    def push(chip, peer, present=None):
+        for (shard, sem), like in zip(shards(chip), (full.at[pl.ds(0, 2)], tags.at[pl.ds(0, 2)])):
+            start(shard, shard, sem, peer, like, present)
 
     def arrived(chip):
         for shard, sem in shards(chip):
             remote(shard, shard, send_sems.at[0], sem, at.sibling).wait_recv()
 
     first, second = at.device(0, 1, 0), at.device(1, 0, 0)
+    above, below = at.me + 8, at.me - 8
+    up, down = at.z + 1 < depth, at.z >= 1
     for copy in local:
         copy.wait()
     for copy in pair:
         copy.wait_recv()
     here = at.chip
-    order = list(range(1, depth))
-    order = sorted(order, key=lambda d: (min(d, depth - d), d))
+    pl.when(up)(lambda: push(here, above, lambda: up))
+    pl.when(down)(lambda: push(here, below, lambda: down))
     push(here, second)
     push(here, first)
-    for d in order:
-        push(here, at.device(0, 0, d))
-    give = remote(tokens, other, send_sems.at[len(sends)], misc_sems.at[2], at.sibling)
-
-    @pl.when(mine == 0)
-    def _():
-        remote(cotangent, other, send_sems.at[len(sends)], misc_sems.at[2], at.sibling).start()
-
-    @pl.when(mine == 1)
-    def _():
-        give.start()
-
-    sends.append(give)
-    for d in [0] + order:
-        if d:
-            chip = at.member(0, 0, d)
-            arrived(chip)
-            push(chip, first)
-            push(chip, second)
-        chip = at.member(0, 1, d)
-        arrived(chip)
-        push(chip, second)
+    swap = misc_sems.at[2]
+    give = remote(tokens, other, send_sems.at[len(sends)], swap, at.sibling)
+    keep = remote(cotangent, other, send_sems.at[len(sends)], swap, at.sibling)
+    on_core(0)(lambda: keep.start())
+    on_core(1)(lambda: give.start())
+    sends.append((tokens, None))
+    facing = here + at.first
+    arrived(facing)
+    push(facing, second)
+    for d in range(1, depth):
+        low, high = at.z >= d, at.z + d < depth
+
+        def from_below(d=d, low=low):
+            arrived(here - 4 * d)
+            pl.when(up)(lambda: push(here - 4 * d, above, lambda: low & up))
+            push(here - 4 * d, first, lambda: low)
+            push(here - 4 * d, second, lambda: low)
+
+        def from_above(d=d, high=high):
+            arrived(here + 4 * d)
+            pl.when(down)(lambda: push(here + 4 * d, below, lambda: high & down))
+            push(here + 4 * d, first, lambda: high)
+            push(here + 4 * d, second, lambda: high)
+
+        def relay_below(d=d, low=low):
+            arrived(facing - 4 * d)
+            push(facing - 4 * d, second, lambda: low)
+
+        def relay_above(d=d, high=high):
+            arrived(facing + 4 * d)
+            push(facing + 4 * d, second, lambda: high)
+
+        pl.when(low)(from_below)
+        pl.when(high)(from_above)
+        pl.when(low)(relay_below)
+        pl.when(high)(relay_above)
     for df in range(2):
-        for d in [0] + order:
+        for d in range(depth):
             arrived(at.member(1, df, d))
     give.wait_recv()
-    for copy in sends:
-        copy.wait_send()
-
-
-def gather_blocks(own, own_tags, tokens, cotangent, devices):
+    for n, (like, present) in enumerate(sends):
+
+        def sent(n=n, like=like):
+            remote(like, like, send_sems.at[n], misc_sems.at[0], at.sibling).wait_send()
+
+        if present is None:
+            sent()
+        else:
+            pl.when(present())(sent)
+
+
+def gather_blocks(own_in, own_out, own_tags, tokens, cotangent, devices):
     chips = devices // 2
     depth = devices // 8
-    sends = 2 * (1 + 2 + (depth - 1) + 2 * (depth - 1) + depth) + 1
+    sends = 2 * (1 + 2 + 2 + 1 + 8 * (depth - 1)) + 1
     anywhere = pl.BlockSpec(memory_space=pl.ANY)
     return pl.pallas_call(
         functools.partial(gather_kernel, devices),
         out_shape=(
-            jax.ShapeDtypeStruct((devices,) + own.shape[1:], own.dtype),
+            jax.ShapeDtypeStruct((devices,) + own_in.shape, own_in.dtype),
             jax.ShapeDtypeStruct((devices,) + own_tags.shape[1:], own_tags.dtype),
             jax.ShapeDtypeStruct(tokens.shape, tokens.dtype),
         ),
-        in_specs=[pl.BlockSpec(memory_space=pltpu.VMEM)] * 2 + [anywhere, anywhere],
+        in_specs=[pl.BlockSpec(memory_space=pltpu.VMEM)] * 3 + [anywhere, anywhere],
         out_specs=(anywhere, anywhere, anywhere),
         scratch_shapes=[
             pltpu.SemaphoreType.DMA((sends,)),
@@ -316,7 +357,7 @@
         ],
         compiler_params=pltpu.CompilerParams(collective_id=0, has_side_effects=True),
         name="gather_blocks",
-    )(own, own_tags, tokens, cotangent)
+    )(own_in, own_out, own_tags, tokens, cotangent)
 
 
 def layer_kernel(devices, per, pos, begin, tokens, cotangent, other, full, out,
@@ -446,7 +487,7 @@
 
     line = sorted(range(1, depth), key=lambda d: (min(d, depth - d), d))
     dist = line[::-1] + [0]
-    order = [(ds, df, d) for ds, df in ((1, 1), (1, 0), (0, 1), (0, 0)) for d in dist]
+    order = [(ds, df, d) for ds in (1, 0) for d in dist for df in (1, 0)]
     for i, (ds, df, dz) in enumerate(order):
         chip = at.member(ds, df, dz)
         parts = []
@@ -534,10 +575,9 @@
 def one_section(tokens, blocks_in, blocks_out, pos_in, pos_out, cotangent):
     devices = lax.axis_size("dp")
     per = blocks_in.shape[1]
-    own = jnp.stack([blocks_in[0], blocks_out[0]])
     places = jnp.concatenate([pos_in, pos_out]).astype(jnp.bfloat16)
     places = jnp.pad(places[:, None, :], ((0, 0), (0, EXTRA - 1), (0, BLOCK - per)))
-    full, tags, other = gather_blocks(own, places, tokens, cotangent, devices)
+    full, tags, other = gather_blocks(blocks_in[0], blocks_out[0], places, tokens, cotangent, devices)
     count = devices * per
     slots = tags[:, 0, :per].astype(jnp.int32)
     starts = per * jnp.arange(devices)[:, None] + jnp.arange(per)[None, :]

time: 146 us -> 127 us (0.87); the launches traced: 143 us -> 127 us
  Pallas kernels: 135 us -> 120 us
  other arithmetic: 5.48 us -> 3.74 us
    pallas_call x1, Pallas kernels: 73 us -> 60.6 us  [layer_sums(): pl.pallas_call(functools.partial(layer_kernel, devices, per), out_shape=j...]
    pallas_call x1, Pallas kernels: 61.5 us -> 59.1 us  [gather_blocks(): pl.pallas_call(functools.partial(gather_kernel, devices), out_shape=(jax....]
    another operation x1 -> x0, other arithmetic: 1.75 us -> none  [one_section(): own = jnp.stack([blocks_in[0], blocks_out[0]])]
where the time goes in v3:
time: 127 us
  Pallas kernels  120 us (94%)
  other arithmetic  3.74 us (3%)
  local copies, waits for them, and re-layouts  2.48 us (2%)
    pallas_call x1, Pallas kernels, layer_sums(): pl.pallas_call(functools.partial(layer_kernel, devices, per), out_shape=j...  60.6 us
    pallas_call x1, Pallas kernels, gather_blocks(): pl.pallas_call(functools.partial(gather_kernel, devices), out_shape=(jax....  59.1 us

profile of v3, /device:TPU:0, one launch (start us, length us, event | category | flops | bytes accessed | tf_op | source)
XLA Modules:
  0.0 126.7 jit_solution(10572539409355804636)
XLA Ops:
  0.6 0.7 convert_bitcast_fusion
  1.3 0.6 fusion.5.own_tags
  1.9 59.1 %gather_blocks.1 = (bf16[32,5,128,128]{3,2,1,0:T(8,128)(2,1)}, bf16[32,16,128]{2,1,0:T(8,128)(2,1)}, bf16[128,8192]{1,0:T(8,128)(2,1)}) custom-call(bf16[5,128,128]{2,1,0:T(8,128)(2,1)} %bitcast.11, bf16[5,128,128]{2,1,0:T(8,128)(2,1)} %bitcast.12, bf16[2,16,128]{2,1,0:T(8,128)(2,1)} %fusion.5.own_tags, bf16[128,8192]{1,0:T(8,128)(2,1)} %tokens.3, ...), custom_call_target="tpu_custom_call" | custom-call | tf_op jit(solution)/shard_map/gather_blocks/pallas_call | solution.py:344
  61.1 0.9 fusion.6
  62.0 0.9 slice_convert_fusion
  62.8 0.7 reshape.74.pos
  63.5 0.1 copy.8
  63.6 0.7 select_reduce_fusion.begin
  64.3 60.6 %layer_sums.1 = bf16[2,640,128]{2,1,0:T(8,128)(2,1)} custom-call(s32[160]{0:T(256)} %reshape.74.pos, s32[256]{0:T(256)} %select_reduce_fusion.begin, bf16[128,8192]{1,0:T(8,128)(2,1)} %tokens.3, bf16[128,8192]{1,0:T(8,128)(2,1)} %cotangent.3, bf16[128,8192]{1,0:T(8,128)(2,1)} %get-tuple-element.6.other, bf16[160,128,128]{2,1,0:T(8,128)(2,1)} %bitcast.10), custom_call_target="tpu_custom_call" | custom-call | tf_op jit(solution)/shard_map/layer_sums/pallas_call | solution.py:542
  124.9 1.7 %fusion.7 = (bf16[1,640,128]{2,1,0:T(8,128)(2,1)}, bf16[1,640,128]{2,1,0:T(8,128)(2,1)}) fusion(bf16[2,640,128]{2,1,0:T(8,128)(2,1)} %layer_sums.1), kind=kLoop, calls=%fused_computation.16 | loop fusion | bytes 655360 | tf_op jit(solution)/shard_map/slice | solution.py:590
  (2 shorter events, 0.0 us)

commit v4 on v3

--- a/solution.py
+++ b/solution.py
@@ -259,14 +259,27 @@
         remote(own_tags.at[0], tags.at[at.me], send_sems.at[0], misc_sems.at[4], at.sibling),
     ]
 
+    per = own_in.shape[0]
+    bulk = full.at[pl.ds(0, 2), pl.ds(0, per - 1)]
+    spare = full.at[pl.ds(0, 2), pl.ds(per - 1, 1)]
+
+    def odd(chip):
+        return full.at[pl.ds(2 * chip, 2), pl.ds(per - 1, 1)]
+
+    def push_odd(chip, peer, present=None):
+        start(odd(chip), odd(chip), chip_sems.at[2, chip], peer, spare, present)
+
+    def odd_arrived(chip):
+        remote(odd(chip), odd(chip), send_sems.at[0], chip_sems.at[2, chip], at.sibling).wait_recv()
+
     def shards(chip):
         return (
-            (full.at[pl.ds(2 * chip, 2)], chip_sems.at[0, chip]),
+            (full.at[pl.ds(2 * chip, 2), pl.ds(0, per - 1)], chip_sems.at[0, chip]),
             (tags.at[pl.ds(2 * chip, 2)], chip_sems.at[1, chip]),
         )
 
     def push(chip, peer, present=None):
-        for (shard, sem), like in zip(shards(chip), (full.at[pl.ds(0, 2)], tags.at[pl.ds(0, 2)])):
+        for (shard, sem), like in zip(shards(chip), (bulk, tags.at[pl.ds(0, 2)])):
             start(shard, shard, sem, peer, like, present)
 
     def arrived(chip):
@@ -285,6 +298,10 @@
     pl.when(down)(lambda: push(here, below, lambda: down))
     push(here, second)
     push(here, first)
+    push_odd(here, first)
+    push_odd(here, second)
+    pl.when(up)(lambda: push_odd(here, above, lambda: up))
+    pl.when(down)(lambda: push_odd(here, below, lambda: down))
     swap = misc_sems.at[2]
     give = remote(tokens, other, send_sems.at[len(sends)], swap, at.sibling)
     keep = remote(cotangent, other, send_sems.at[len(sends)], swap, at.sibling)
@@ -294,6 +311,29 @@
     facing = here + at.first
     arrived(facing)
     push(facing, second)
+    plane = [here, facing, here + at.second, facing + at.second]
+    for q in plane[1:]:
+        odd_arrived(q)
+        if q is facing:
+            push_odd(q, second)
+        pl.when(up)(lambda q=q: push_odd(q, above, lambda: up))
+        pl.when(down)(lambda q=q: push_odd(q, below, lambda: down))
+
+    def odd_line(d):
+        low, high = at.z >= d, at.z + d < depth
+        for q in plane:
+
+            def odd_below(q=q):
+                odd_arrived(q - 4 * d)
+                pl.when(up)(lambda: push_odd(q - 4 * d, above, lambda: low & up))
+
+            def odd_above(q=q):
+                odd_arrived(q + 4 * d)
+                pl.when(down)(lambda: push_odd(q + 4 * d, below, lambda: high & down))
+
+            pl.when(low)(odd_below)
+            pl.when(high)(odd_above)
+
     for d in range(1, depth):
         low, high = at.z >= d, at.z + d < depth
 
@@ -321,6 +361,10 @@
         pl.when(high)(from_above)
         pl.when(low)(relay_below)
         pl.when(high)(relay_above)
+        if d > 1:
+            odd_line(d - 1)
+    if depth > 1:
+        odd_line(depth - 1)
     for df in range(2):
         for d in range(depth):
             arrived(at.member(1, df, d))
@@ -339,7 +383,7 @@
 def gather_blocks(own_in, own_out, own_tags, tokens, cotangent, devices):
     chips = devices // 2
     depth = devices // 8
-    sends = 2 * (1 + 2 + 2 + 1 + 8 * (depth - 1)) + 1
+    sends = 2 * (1 + 2 + 2 + 1 + 8 * (depth - 1)) + 1 + 11 + 8 * (depth - 1)
     anywhere = pl.BlockSpec(memory_space=pl.ANY)
     return pl.pallas_call(
         functools.partial(gather_kernel, devices),
@@ -352,7 +396,7 @@
         out_specs=(anywhere, anywhere, anywhere),
         scratch_shapes=[
             pltpu.SemaphoreType.DMA((sends,)),
-            pltpu.SemaphoreType.DMA((2, chips)),
+            pltpu.SemaphoreType.DMA((3, chips)),
             pltpu.SemaphoreType.DMA((5,)),
         ],
         compiler_params=pltpu.CompilerParams(collective_id=0, has_side_effects=True),

time: 127 us -> 125 us (0.984)
  Pallas kernels: 120 us -> 118 us
where the time goes in v4:
time: 125 us
  Pallas kernels  118 us (94%)
  other arithmetic  3.74 us (3%)
  local copies, waits for them, and re-layouts  2.48 us (2%)
    pallas_call x1, Pallas kernels, layer_sums(): pl.pallas_call(functools.partial(layer_kernel, devices, per), out_shape=j...  59.4 us
    pallas_call x1, Pallas kernels, gather_blocks(): pl.pallas_call(functools.partial(gather_kernel, devices), out_shape=(jax....  58.4 us

profile of v4, /device:TPU:0, one launch (start us, length us, event | category | flops | bytes accessed | tf_op | source)
XLA Modules:
  0.0 124.7 jit_solution(14927611514429642438)
XLA Ops:
  0.6 0.7 convert_bitcast_fusion
  1.3 0.6 fusion.5.own_tags
  1.9 58.4 %gather_blocks.1 = (bf16[32,5,128,128]{3,2,1,0:T(8,128)(2,1)}, bf16[32,16,128]{2,1,0:T(8,128)(2,1)}, bf16[128,8192]{1,0:T(8,128)(2,1)}) custom-call(bf16[5,128,128]{2,1,0:T(8,128)(2,1)} %bitcast.11, bf16[5,128,128]{2,1,0:T(8,128)(2,1)} %bitcast.12, bf16[2,16,128]{2,1,0:T(8,128)(2,1)} %fusion.5.own_tags, bf16[128,8192]{1,0:T(8,128)(2,1)} %tokens.3, ...), custom_call_target="tpu_custom_call" | custom-call | tf_op jit(solution)/shard_map/gather_blocks/pallas_call | solution.py:388
  60.4 0.9 fusion.6
  61.3 0.9 slice_convert_fusion
  62.1 0.7 reshape.74.pos
  62.8 0.1 copy.8
  62.9 0.7 select_reduce_fusion.begin
  63.6 59.4 %layer_sums.1 = bf16[2,640,128]{2,1,0:T(8,128)(2,1)} custom-call(s32[160]{0:T(256)} %reshape.74.pos, s32[256]{0:T(256)} %select_reduce_fusion.begin, bf16[128,8192]{1,0:T(8,128)(2,1)} %tokens.3, bf16[128,8192]{1,0:T(8,128)(2,1)} %cotangent.3, bf16[128,8192]{1,0:T(8,128)(2,1)} %get-tuple-element.6.other, bf16[160,128,128]{2,1,0:T(8,128)(2,1)} %bitcast.10), custom_call_target="tpu_custom_call" | custom-call | tf_op jit(solution)/shard_map/layer_sums/pallas_call | solution.py:586
  123.0 1.7 %fusion.7 = (bf16[1,640,128]{2,1,0:T(8,128)(2,1)}, bf16[1,640,128]{2,1,0:T(8,128)(2,1)}) fusion(bf16[2,640,128]{2,1,0:T(8,128)(2,1)} %layer_sums.1), kind=kLoop, calls=%fused_computation.16 | loop fusion | bytes 655360 | tf_op jit(solution)/shard_map/slice | solution.py:634
  (2 shorter events, 0.0 us)

commit v5 on v4

--- a/solution.py
+++ b/solution.py
@@ -405,7 +405,7 @@
 
 
 def layer_kernel(devices, per, pos, begin, tokens, cotangent, other, full, out,
-                 blocks, rows, mat_a, mat_b, grads, middle, middle_got, inverse,
+                 blocks, rows, mat_a, mat_b, grads, middle, packed, middle_got, inverse,
                  held, second_got, first_got, line_got, last_got,
                  load_sems, send_sems, second_sems, first_sems, line_sems, pair_sems):
     at = Place(devices)
@@ -496,14 +496,15 @@
         middle[...] = dact
 
     wait_peers()
-    start(middle, middle_got, pair_sems.at[0], at.sibling).wait_recv()
+    packed[...] = middle[...].astype(jnp.bfloat16)
+    start(packed, middle_got, pair_sems.at[0], at.sibling).wait_recv()
     across = (((0,), (0,)), ((), ()))
 
     @pl.when(mine == 0)
     def _():
         pre = middle[...]
         sig = jax.nn.sigmoid(pre)
-        dpre = middle_got[...] * sig * (1.0 + pre * (1.0 - sig))
+        dpre = middle_got[...].astype(jnp.float32) * sig * (1.0 + pre * (1.0 - sig))
         dpre = (dpre * inverse[:, :1]).astype(jnp.bfloat16)
         for k in chunks:
             part = lax.dot_general(
@@ -517,7 +518,7 @@
 
     @pl.when(mine == 1)
     def _():
-        pre = middle_got[...]
+        pre = middle_got[...].astype(jnp.float32)
         act = (pre * jax.nn.sigmoid(pre)).astype(jnp.bfloat16)
         for k in chunks:
             part = lax.dot_general(
@@ -595,7 +596,8 @@
             vmem((RANK, width), bf16),
             vmem((width * RANK // (BLOCK * BLOCK) + 1, BLOCK, BLOCK), bf16),
             vmem((2 * count, RANK), f32),
-            vmem((2 * count, RANK), f32),
+            vmem((2 * count, RANK), bf16),
+            vmem((2 * count, RANK), bf16),
             vmem((2 * count, BLOCK), f32),
             vmem((chips,) + shard, bf16),
             vmem((2 * depth,) + shard, bf16),

time: 125 us -> 125 us (level)
  no operation moved by 1% of the time
where the time goes in v5:
time: 125 us; the launch traced here: 124 us
  Pallas kernels  118 us (94%)
  other arithmetic  3.74 us (3%)
  local copies, waits for them, and re-layouts  2.48 us (2%)
    pallas_call x1, Pallas kernels, layer_sums(): pl.pallas_call(functools.partial(layer_kernel, devices, per), out_shape=j...  59.1 us
    pallas_call x1, Pallas kernels, gather_blocks(): pl.pallas_call(functools.partial(gather_kernel, devices), out_shape=(jax....  58.4 us

profile of v5, /device:TPU:0, one launch (start us, length us, event | category | flops | bytes accessed | tf_op | source)
XLA Modules:
  0.0 124.4 jit_solution(15410621892377549434)
XLA Ops:
  0.6 0.7 convert_bitcast_fusion
  1.3 0.6 fusion.5.own_tags
  1.9 58.4 %gather_blocks.1 = (bf16[32,5,128,128]{3,2,1,0:T(8,128)(2,1)}, bf16[32,16,128]{2,1,0:T(8,128)(2,1)}, bf16[128,8192]{1,0:T(8,128)(2,1)}) custom-call(bf16[5,128,128]{2,1,0:T(8,128)(2,1)} %bitcast.11, bf16[5,128,128]{2,1,0:T(8,128)(2,1)} %bitcast.12, bf16[2,16,128]{2,1,0:T(8,128)(2,1)} %fusion.5.own_tags, bf16[128,8192]{1,0:T(8,128)(2,1)} %tokens.3, ...), custom_call_target="tpu_custom_call" | custom-call | tf_op jit(solution)/shard_map/gather_blocks/pallas_call | solution.py:388
  60.4 0.9 fusion.6
  61.3 0.9 slice_convert_fusion
  62.1 0.7 reshape.74.pos
  62.8 0.1 copy.8
  62.9 0.7 select_reduce_fusion.begin
  63.6 59.1 %layer_sums.1 = bf16[2,640,128]{2,1,0:T(8,128)(2,1)} custom-call(s32[160]{0:T(256)} %reshape.74.pos, s32[256]{0:T(256)} %select_reduce_fusion.begin, bf16[128,8192]{1,0:T(8,128)(2,1)} %tokens.3, bf16[128,8192]{1,0:T(8,128)(2,1)} %cotangent.3, bf16[128,8192]{1,0:T(8,128)(2,1)} %get-tuple-element.6.other, bf16[160,128,128]{2,1,0:T(8,128)(2,1)} %bitcast.10), custom_call_target="tpu_custom_call" | custom-call | tf_op jit(solution)/shard_map/layer_sums/pallas_call | solution.py:587
  122.7 1.7 %fusion.7 = (bf16[1,640,128]{2,1,0:T(8,128)(2,1)}, bf16[1,640,128]{2,1,0:T(8,128)(2,1)}) fusion(bf16[2,640,128]{2,1,0:T(8,128)(2,1)} %layer_sums.1), kind=kLoop, calls=%fused_computation.16 | loop fusion | bytes 655360 | tf_op jit(solution)/shard_map/slice | solution.py:636
  (2 shorter events, 0.0 us)
